TPU v7x, 512 devices: a whole 4x4x16 slice. The times are simulated.
512 devices in a mesh: dp: 16 (over x_hi, y, core), seq: 32 (over x_lo, z).
Axes of the slice: x: 4 (x_hi: 2, x_lo: 2; x = x_hi * 2 + x_lo), y: 4, z: 16, core: 2. Of those that a mesh axis runs over, the one named last changes fastest.
Arguments:
- queries: bfloat16 [16, 32768, 128], P('dp', 'seq'), may hold values from -6 to 6
- key_vectors: bfloat16 [16, 32768, 128], P('dp', 'seq'), may hold values from -6 to 6
- value_vectors: bfloat16 [16, 32768, 128], P('dp', 'seq'), may hold values from -6 to 6
- out_grad: bfloat16 [16, 32768, 128], P('dp', 'seq'), may hold values from -6 to 6
- log_decay: float32 [16, 1, 32768], P('dp', None, 'seq'), may hold values from -0.8 to 0, as said below
- prev_grads: bfloat16 [16, 1024, 6144], P('dp', 'seq'), may hold values from -6 to 6
Outputs:
- attn_out: bfloat16 [16, 32768, 128], P('dp', 'seq')
- grad_query: bfloat16 [16, 32768, 128], P('dp', 'seq')
- grad_key: bfloat16 [16, 32768, 128], P('dp', 'seq')
- grad_value: bfloat16 [16, 32768, 128], P('dp', 'seq')
- grad_shard: float32 [1024, 6144], P('seq', 'dp')
Inputs may be any that keep to these rules, and one draw needn't show every extreme that they name: `log_decay`: every entry is negative.
All inputs are finite; a program needn't handle non-finite values.
Results may differ from a plain program's by a relative error of at most 0.012.
Values may be sent and summed in bfloat16 or wider, within the bound.
A program may use at most 64 MiB of HBM per device.

v0:
```python
import jax
import jax.numpy as jnp
from jax import lax
from jax.sharding import PartitionSpec as P

BLK = 512


NORM_EPS = 1e-06
FULL_PRECISION = lax.Precision.HIGHEST


def product(left, right):
    return jnp.dot(left, right, precision=FULL_PRECISION, preferred_element_type=jnp.float32)


def decay_mask(running):
    spread = running[:, None] - running[None, :]
    lower_mask = jnp.tril(jnp.ones(spread.shape, dtype=bool))
    return jnp.where(lower_mask, jnp.exp(jnp.minimum(spread, 0.0)), 0.0)


def forward_local(query_head, key_head, value_head, decay_head):
    head_width = query_head.shape[-1]

    def advance(carried, block_inputs):
        query_block, key_block, value_block, decay_block = block_inputs
        running = jnp.cumsum(decay_block)
        scores = jnp.dot(query_block, key_block.T, preferred_element_type=jnp.float32) * decay_mask(
            running
        )
        query_wide = query_block.astype(jnp.float32)
        key_wide = key_block.astype(jnp.float32)
        value_wide = value_block.astype(jnp.float32)
        block_out = product(scores, value_wide) + jnp.exp(running)[:, None] * product(
            query_wide, carried
        )
        weights = jnp.exp(running[-1] - running)
        updated = jnp.exp(running[-1]) * carried + product(
            (key_wide * weights[:, None]).T, value_wide
        )
        return (updated, (block_out, carried))

    return lax.scan(
        advance,
        jnp.zeros((head_width, head_width), jnp.float32),
        (query_head, key_head, value_head, decay_head),
    )


def backward_local(query_head, key_head, value_head, dattn_head, decay_head, start_head):
    head_width = query_head.shape[-1]

    def retreat(later_sum, block_inputs):
        query_block, key_block, value_block, dattn_block, decay_block, carried = block_inputs
        running = jnp.cumsum(decay_block)
        decay_weights = decay_mask(running)
        scores = (
            jnp.dot(query_block, key_block.T, preferred_element_type=jnp.float32) * decay_weights
        )
        query_wide = query_block.astype(jnp.float32)
        key_wide = key_block.astype(jnp.float32)
        value_wide = value_block.astype(jnp.float32)
        dscores = product(dattn_block, value_wide.T) * decay_weights
        lead_decay = jnp.exp(running)[:, None]
        tail_decay = jnp.exp(running[-1] - running)[:, None]
        grad_q = product(dscores, key_wide) + lead_decay * product(dattn_block, carried.T)
        grad_k = product(dscores.T, query_wide) + tail_decay * product(value_wide, later_sum.T)
        grad_v = product(scores.T, dattn_block) + tail_decay * product(key_wide, later_sum)
        updated = jnp.exp(running[-1]) * later_sum + product(
            (query_wide * lead_decay).T, dattn_block
        )
        return (updated, (grad_q, grad_k, grad_v))

    return lax.scan(
        retreat,
        jnp.zeros((head_width, head_width), jnp.float32),
        (query_head, key_head, value_head, dattn_head, decay_head, start_head),
        reverse=True,
    )


def weigh_fold(block_logs, own_index, upward, running_sum, shard_part):
    summed_logs = jnp.cumsum(block_logs, axis=0)
    own_cum = lax.dynamic_index_in_dim(summed_logs, own_index, 0, keepdims=False)
    own_log = lax.dynamic_index_in_dim(block_logs, own_index, 0, keepdims=False)
    piece_count = shard_part.shape[0]
    token_offsets = jnp.arange(piece_count, dtype=jnp.int32)
    if upward:
        spread = summed_logs - block_logs - own_cum[None, :]
        usable = token_offsets > own_index
    else:
        spread = own_cum[None, :] - own_log[None, :] - summed_logs
        usable = token_offsets < own_index
    weights = jnp.where(usable[:, None], jnp.exp(jnp.minimum(spread, 0.0)), 0.0)
    return running_sum + jnp.einsum("nh,nhab->hab", weights, shard_part, precision=FULL_PRECISION)


def local(queries, key_vectors, value_vectors, out_grad, log_decay, prev_grads):
    row_count = queries.shape[1]
    head_count = log_decay.shape[1]
    head_width = queries.shape[2] // head_count
    block_count = row_count // BLK

    def by_head(tensor):
        return tensor[0].reshape(row_count, head_count, head_width).transpose(1, 0, 2)

    def by_block(tensor):
        return tensor.reshape(head_count, block_count, BLK, head_width)

    def to_rows(tensor):
        return (
            tensor.transpose(1, 0, 2)
            .reshape(1, row_count, head_count * head_width)
            .astype(jnp.bfloat16)
        )

    query_heads = by_head(queries)
    key_heads = by_head(key_vectors)
    value_heads = by_head(value_vectors)
    decay_rows = log_decay[0]
    decay_blocks = decay_rows.reshape(head_count, block_count, BLK)
    cumulative = jnp.cumsum(decay_rows, axis=1)
    log_total = cumulative[:, -1]
    local_state, (local_out, block_starts) = jax.vmap(forward_local)(
        by_block(query_heads), by_block(key_heads), by_block(value_heads), decay_blocks
    )
    identity = (
        jnp.zeros((head_count,), jnp.float32),
        jnp.zeros((head_count, head_width, head_width), jnp.float32),
    )
    own_index = lax.axis_index("seq")
    block_logs = lax.all_gather(log_total[None], "seq", axis=0, tiled=True)
    incoming = weigh_fold(
        block_logs,
        own_index,
        False,
        identity[1],
        lax.all_gather(local_state[None].astype(jnp.bfloat16), "seq", axis=0, tiled=True).astype(
            jnp.float32
        ),
    )
    query_wide = query_heads.astype(jnp.float32)
    key_wide = key_heads.astype(jnp.float32)
    value_wide = value_heads.astype(jnp.float32)
    lead_decay = jnp.exp(cumulative)[:, :, None]
    attention = local_out.reshape(head_count, row_count, head_width) + lead_decay * jnp.einsum(
        "hta,hab->htb", query_wide, incoming, precision=FULL_PRECISION
    )
    norm_ratio = lax.rsqrt(jnp.mean(attention * attention, axis=-1, keepdims=True) + NORM_EPS)
    attn_out = to_rows(attention * norm_ratio)
    cotangent = by_head(out_grad).astype(jnp.float32)
    cubed = norm_ratio * norm_ratio * norm_ratio
    dattn = (
        norm_ratio * cotangent
        - cubed / head_width * jnp.sum(cotangent * attention, axis=-1, keepdims=True) * attention
    )
    local_future, (grad_q_local, grad_k_local, grad_v_local) = jax.vmap(backward_local)(
        by_block(query_heads),
        by_block(key_heads),
        by_block(value_heads),
        by_block(dattn),
        decay_blocks,
        block_starts,
    )
    outgoing = weigh_fold(
        block_logs,
        own_index,
        True,
        identity[1],
        lax.all_gather(local_future[None].astype(jnp.bfloat16), "seq", axis=0, tiled=True).astype(
            jnp.float32
        ),
    )
    tail_decay = jnp.exp(log_total[:, None] - cumulative)[:, :, None]
    grad_query = grad_q_local.reshape(head_count, row_count, head_width) + lead_decay * jnp.einsum(
        "htb,hab->hta", dattn, incoming, precision=FULL_PRECISION
    )
    grad_key = grad_k_local.reshape(head_count, row_count, head_width) + tail_decay * jnp.einsum(
        "htb,hab->hta", value_wide, outgoing, precision=FULL_PRECISION
    )
    grad_value = grad_v_local.reshape(head_count, row_count, head_width) + tail_decay * jnp.einsum(
        "hta,hab->htb", key_wide, outgoing, precision=FULL_PRECISION
    )
    summed = lax.psum_scatter(
        prev_grads.astype(jnp.float32).astype(jnp.bfloat16), "dp", scatter_dimension=2, tiled=True
    ).astype(jnp.float32)
    return (attn_out, to_rows(grad_query), to_rows(grad_key), to_rows(grad_value), summed[0])


def solution(mesh):
    return jax.shard_map(
        local,
        mesh=mesh,
        in_specs=(
            P("dp", "seq", None),
            P("dp", "seq", None),
            P("dp", "seq", None),
            P("dp", "seq", None),
            P("dp", None, "seq"),
            P("dp", "seq", None),
        ),
        out_specs=(
            P("dp", "seq", None),
            P("dp", "seq", None),
            P("dp", "seq", None),
            P("dp", "seq", None),
            P("seq", "dp"),
        ),
        check_vma=False,
    )
```

profile of v0, /device:TPU:6, one launch (start us, length us, event | category | flops | bytes accessed | tf_op | source)
XLA Modules:
  0.0 324.1 jit_solution(16678804130265049411)
XLA Ops:
  8.1 15.7 %while.36 = (s32[]{:T(128)}, f32[1,128,128]{2,1,0:T(8,128)S(1)}, f32[2,1,512,128]{3,2,1,0:T(8,128)S(1)}, f32[2,1,128,128]{3,2,1,0:T(8,128)S(1)}, f32[2,1,512]{2,...) while((s32[]{:T(128)}, f32[1,128,128]{2,1,0:T(8,128)S(1)}, ...), condition=%wide.region_3.4_spmd.clone, body=%wide.region_0.3_spmd.clone.sunk | while | flops 672809472 | bytes 7176599 | solution.py:44
  8.2 0.8 constant_dynamic-slice_fusion.5
  9.2 0.6 slice.78
  10.2 0.6 slice.79
  12.3 1.3 convolution_multiply_fusion.14
  13.6 1.5 fusion.176
  15.4 0.5 fusion.175
  16.0 0.8 constant_dynamic-slice_fusion.5
  17.1 0.6 slice.78
  18.1 0.6 slice.79
  20.1 1.3 convolution_multiply_fusion.14
  21.4 1.5 fusion.176
  23.2 0.5 fusion.175
  23.8 0.7 convert_element_type.117
  24.6 6.1 %copy.49 = bf16[1,32,6144]{1,0,2:T(2,128)(2,1)S(1)} copy(bf16[1,32,6144]{2,1,0:T(8,128)(2,1)} %param.15) | data formatting | bytes 786432
  30.7 1.4 copy.57
  32.7 0.6 slice.60
  33.5 0.6 slice.61
  34.1 1.3 dynamic-slice
  36.7 0.7 bitcast_dynamic-update-slice_fusion.1
  37.4 69.9 %all-reduce = f32[32]{0:T(128)S(1)} all-reduce(f32[32]{0:T(128)S(1)} %bitcast_dynamic-update-slice_fusion.1), channel_id=1, replica_groups=mesh['dp'=16,'seq'=32] {'seq'}, use_global_device_ids=true, to_apply=%add | all-reduce | flops 32 | bytes 256
  107.3 0.6 dynamic-slice.1
  108.0 1.1 copy.33
  109.1 1.2 copy.45
  110.4 1.2 fusion.120
  111.6 2.0 select_reduce_fusion
  113.6 46.9 %all-gather.5.cloned.1.call-done = bf16[32,128,128]{2,1,0:T(8,128)(2,1)} async-done(((bf16[1,128,128]{2,1,0:T(8,128)(2,1)}), bf16[32,128,128]{2,1,0:T(8,128)(2,1)}) %all-gather.5.cloned.1.call-update) | async-done | bytes 1048592 | tf_op jit(solution)/shard_map/all_gather | solution.py:139
  160.5 2.2 fusion.105
  162.7 0.5 fusion.108
  163.7 0.8 broadcast.304
  164.5 21.6 %while.37 = (s32[]{:T(128)}, f32[1,128,128]{2,1,0:T(8,128)S(1)}, f32[2,1,512,128]{3,2,1,0:T(8,128)}, f32[2,1,512,128]{3,2,1,0:T(8,128)S(1)}, f32[2,1,512,128]{3,...) while((s32[]{:T(128)}, f32[1,128,128]{2,1,0:T(8,128)S(1)}, ...), condition=%wide.region_12.13_spmd.clone, body=%wide.region_9.12_spmd.clone.sunk | while | flops 2083668480 | bytes 14791102 | solution.py:75
  164.9 0.6 slice.82
  165.6 0.7 reduce-window.55
  166.3 0.7 slice_bitcast_fusion.6
  167.1 0.6 slice.83
  169.1 0.6 convolution_multiply_fusion.15
  169.8 1.0 fusion.199
  170.8 0.6 fusion.197
  171.4 0.4 fusion.198
  172.2 0.3 convolution_multiply_fusion.16
  172.5 1.8 fusion.201
  174.6 0.7 fusion.196
  175.7 0.6 slice.82
  176.4 0.7 reduce-window.55
  177.1 0.7 slice_bitcast_fusion.6
  177.9 0.6 slice.83
  179.9 0.7 convolution_multiply_fusion.15
  180.6 1.0 fusion.199
  181.6 0.6 fusion.197
  182.2 0.4 fusion.198
  183.3 1.8 fusion.201
  185.4 0.7 fusion.196
  186.2 0.6 convert_element_type.124
  186.8 1.0 reshape_bitcast_fusion
  187.9 0.6 bitcast_convert_fusion
  188.6 0.7 fusion.110
  189.3 0.8 copy.38
  190.6 1.7 fusion.102
  192.3 119.6 %all-gather.7.cloned.1.call-done = bf16[32,128,128]{2,1,0:T(8,128)(2,1)} async-done(((bf16[1,128,128]{2,1,0:T(8,128)(2,1)}), bf16[32,128,128]{2,1,0:T(8,128)(2,1)}) %all-gather.7.cloned.1.call-update) | async-done | bytes 1048592 | tf_op jit(solution)/shard_map/all_gather | solution.py:171
  311.9 2.2 fusion.103
  314.1 0.4 fusion.100
  314.6 0.8 copy.40
  315.4 0.4 fusion.101
  315.8 0.8 copy.39
  (110 shorter events, 7.2 us)
Async XLA Ops:
  8.0 152.5 %all-gather.5.cloned.1.call-start = ((), (), s32[]{:S(2)}) async-start(), calls=%async_computation.1 | async-start | bytes 1081344 | tf_op jit(solution)/shard_map/all_gather | solution.py:139
  8.1 7.0 %copy-start.4 = (bf16[2,1,512,128]{3,2,1,0:T(8,128)(2,1)S(1)}, bf16[2,1,512,128]{3,2,1,0:T(8,128)(2,1)}, u32[]{:S(2)}) copy-start(bf16[2,1,512,128]{3,2,1,0:T(8,128)(2,1)} %get-tuple-element.592) | copy-start | bytes 786436 | tf_op jit(solution)/shard_map/vmap()/while
  8.1 7.2 %copy-start = (bf16[2,1,512,128]{3,2,1,0:T(8,128)(2,1)S(1)}, bf16[2,1,512,128]{3,2,1,0:T(8,128)(2,1)}, u32[]{:S(2)}) copy-start(bf16[2,1,512,128]{3,2,1,0:T(8,128)(2,1)} %get-tuple-element.590) | copy-start | bytes 786436 | tf_op jit(solution)/shard_map/vmap()/while
  8.1 7.2 %copy-start.2 = (bf16[2,1,512,128]{3,2,1,0:T(8,128)(2,1)S(1)}, bf16[2,1,512,128]{3,2,1,0:T(8,128)(2,1)}, u32[]{:S(2)}) copy-start(bf16[2,1,512,128]{3,2,1,0:T(8,128)(2,1)} %get-tuple-element.591) | copy-start | bytes 786436 | tf_op jit(solution)/shard_map/vmap()/while
  16.0 7.0 %copy-start.4 = (bf16[2,1,512,128]{3,2,1,0:T(8,128)(2,1)S(1)}, bf16[2,1,512,128]{3,2,1,0:T(8,128)(2,1)}, u32[]{:S(2)}) copy-start(bf16[2,1,512,128]{3,2,1,0:T(8,128)(2,1)} %get-tuple-element.592) | copy-start | bytes 786436 | tf_op jit(solution)/shard_map/vmap()/while
  16.0 7.3 %copy-start = (bf16[2,1,512,128]{3,2,1,0:T(8,128)(2,1)S(1)}, bf16[2,1,512,128]{3,2,1,0:T(8,128)(2,1)}, u32[]{:S(2)}) copy-start(bf16[2,1,512,128]{3,2,1,0:T(8,128)(2,1)} %get-tuple-element.590) | copy-start | bytes 786436 | tf_op jit(solution)/shard_map/vmap()/while
  16.0 7.2 %copy-start.2 = (bf16[2,1,512,128]{3,2,1,0:T(8,128)(2,1)S(1)}, bf16[2,1,512,128]{3,2,1,0:T(8,128)(2,1)}, u32[]{:S(2)}) copy-start(bf16[2,1,512,128]{3,2,1,0:T(8,128)(2,1)} %get-tuple-element.591) | copy-start | bytes 786436 | tf_op jit(solution)/shard_map/vmap()/while
  23.8 0.8 copy-start.9
  23.8 6.9 %copy-start.10 = (f32[2,1,128,128]{3,2,1,0:T(8,128)}, f32[2,1,128,128]{3,2,1,0:T(8,128)S(1)}, u32[]{:S(2)}) copy-start(f32[2,1,128,128]{3,2,1,0:T(8,128)S(1)} %get-tuple-element.606) | copy-start | bytes 393220
  24.6 162.2 %reduce-scatter.4.cloned.1.call-start = ((), (), s32[]{:S(2)}) async-start(), calls=%async_computation.3 | async-start | bytes 1671168
  30.7 1.5 copy-start.12
  32.1 130.6 %copy-start.5 = (bf16[2,1,512,128]{3,2,1,0:T(8,128)(2,1)S(1)}, bf16[2,1,512,128]{3,2,1,0:T(8,128)(2,1)}, u32[]{:S(2)}) copy-start(bf16[2,1,512,128]{3,2,1,0:T(8,128)(2,1)} %get-tuple-element.645) | copy-start | bytes 786436
  32.1 279.8 %all-gather.7.cloned.1.call-start = ((), (), s32[]{:S(2)}) async-start(), calls=%async_computation.2 | async-start | bytes 1081344 | tf_op jit(solution)/shard_map/all_gather | solution.py:171
  107.3 56.1 %copy-start.13 = (f32[1024]{0:T(1024)}, f32[1024]{0:T(1024)S(1)}, u32[]{:S(2)}) copy-start(f32[1024]{0:T(1024)S(1)} %get-tuple-element.432) | copy-start | bytes 12292
  162.7 1.9 copy-start.1
  162.7 1.8 copy-start.3
  163.3 1.3 copy-start.15
  166.3 5.1 %copy-start.6 = (f32[2,1,512,128]{3,2,1,0:T(8,128)S(1)}, f32[2,1,512,128]{3,2,1,0:T(8,128)}, u32[]{:S(2)}) copy-start(f32[2,1,512,128]{3,2,1,0:T(8,128)} %get-tuple-element.612) | copy-start | bytes 1572868 | tf_op jit(solution)/shard_map/vmap()/while
  166.3 5.1 %copy-start.11 = (f32[2,1,128,128]{3,2,1,0:T(8,128)S(1)}, f32[2,1,128,128]{3,2,1,0:T(8,128)}, u32[]{:S(2)}) copy-start(f32[2,1,128,128]{3,2,1,0:T(8,128)} %get-tuple-element.634) | copy-start | bytes 393220 | tf_op jit(solution)/shard_map/vmap()/while
  171.8 3.5 %copy-start.7 = (f32[2,1,512,128]{3,2,1,0:T(8,128)}, f32[2,1,512,128]{3,2,1,0:T(8,128)S(1)}, u32[]{:S(2)}) copy-start(f32[2,1,512,128]{3,2,1,0:T(8,128)S(1)} %fusion.198) | copy-start | bytes 1572868 | tf_op jit(solution)/shard_map/vmap()/while
  177.1 5.1 %copy-start.6 = (f32[2,1,512,128]{3,2,1,0:T(8,128)S(1)}, f32[2,1,512,128]{3,2,1,0:T(8,128)}, u32[]{:S(2)}) copy-start(f32[2,1,512,128]{3,2,1,0:T(8,128)} %get-tuple-element.612) | copy-start | bytes 1572868 | tf_op jit(solution)/shard_map/vmap()/while
  177.1 5.1 %copy-start.11 = (f32[2,1,128,128]{3,2,1,0:T(8,128)S(1)}, f32[2,1,128,128]{3,2,1,0:T(8,128)}, u32[]{:S(2)}) copy-start(f32[2,1,128,128]{3,2,1,0:T(8,128)} %get-tuple-element.634) | copy-start | bytes 393220 | tf_op jit(solution)/shard_map/vmap()/while
  182.6 3.5 %copy-start.7 = (f32[2,1,512,128]{3,2,1,0:T(8,128)}, f32[2,1,512,128]{3,2,1,0:T(8,128)S(1)}, u32[]{:S(2)}) copy-start(f32[2,1,512,128]{3,2,1,0:T(8,128)S(1)} %fusion.198) | copy-start | bytes 1572868 | tf_op jit(solution)/shard_map/vmap()/while
  186.1 4.4 %copy-start.8 = (f32[2,1,512,128]{3,2,1,0:T(8,128)S(1)}, f32[2,1,512,128]{3,2,1,0:T(8,128)}, u32[]{:S(2)}) copy-start(f32[2,1,512,128]{3,2,1,0:T(8,128)} %get-tuple-element.272) | copy-start | bytes 1572868
  186.1 4.4 %copy-start.14 = (f32[1024]{0:T(1024)S(1)}, f32[1024]{0:T(1024)}, u32[]{:S(2)}) copy-start(f32[1024]{0:T(1024)} %copy-done.13) | copy-start | bytes 12292
  186.2 125.8 %copy-start.16 = (f32[32]{0:T(128)S(1)}, f32[32]{0:T(128)}, u32[]{:S(2)}) copy-start(f32[32]{0:T(128)} %get-tuple-element.387) | copy-start | bytes 388
Sparse Core Ops, SparseCore 0:
  24.6 135.8 all-gather.4
  186.9 124.9 all-gather.6
Sparse Core Ops, SparseCore 1:
  32.2 95.8 reduce-scatter.3
where the time goes:
time: 326 us; the launch traced here: 324 us
  waiting for transfers between devices  167 us (51%)
  blocking collectives  69.9 us (21%)
  local copies, waits for them, and re-layouts  27.9 us (9%)
  matrix products  26.8 us (8%)
  between operations  17.1 us (5%)
  other arithmetic  9.85 us (3%)
  loops' own time  5.81 us (2%)
    all_gather x1, waiting for transfers between devices, local(): lax.all_gather(local_future[None].astype(jnp.bfloat16), 'seq', axis=0, ti...  120 us
    unnamed x1, blocking collectives  69.9 us
    all_gather x1, waiting for transfers between devices, local(): lax.all_gather(local_state[None].astype(jnp.bfloat16), 'seq', axis=0, til...  46.9 us
    dot_general x22, matrix products, product(): jnp.dot(left, right, precision=FULL_PRECISION, preferred_element_type=jnp...  16.3 us
    unnamed x36, local copies, waits for them, and re-layouts  15.1 us
  transfers between devices with their start and end apart: 3, of which 2 were waited for; matrix products, arithmetic and copies ran while one was open for 14% of the time, Pallas kernels for 0%

commit v1 on v0

v1 whole, which is shorter than its diff:
```python
import functools

import jax
import jax.numpy as jnp
from jax import lax
from jax.experimental import pallas as pl
from jax.experimental.pallas import tpu as pltpu
from jax.sharding import PartitionSpec as P

NORM_EPS = 1e-06
MESH = pl.DeviceIdType.MESH
EXACT = lax.Precision.HIGHEST
F32 = jnp.float32
BF16 = jnp.bfloat16

ROWS = 256
LANES = 128
X_PARTS = 2
QUAD = 4
PIECES = X_PARTS * QUAD


def dot(left, right, left_dim=1, right_dim=0):
    return lax.dot_general(
        left, right, (((left_dim,), (right_dim,)), ((), ())), preferred_element_type=F32
    )


def wait_bytes(ref, sem):
    pltpu.make_async_copy(ref, ref, sem).wait()


def kernel(
    n_dp, n_seq,
    q_hbm, k_hbm, v_hbm, dy_hbm, ld_hbm, pg_hbm,
    out_hbm, gq_hbm, gk_hbm, gv_hbm, gs_hbm,
    q, k, v, dy, ld, out, gq, gk, gv, gs,
    col, lead, tail, mask, scores, keyed, attn, dattn, gkl, gvl,
    state, gathered, prefix, incoming, state2, gathered2, prefix2, outgoing,
    own_log, logs, parts,
    load_sem, store_sem, part_send, part_recv, log_send, log_recv, own_sem,
    s1_send, s1_recv, s2_send, s2_recv, r1_send, r1_recv, r2_send, r2_recv,
):
    tokens, width = q.shape
    blocks = tokens // ROWS
    chunks = tokens // LANES
    n_z = n_seq // X_PARTS
    half = n_z // 2
    my_dp = lax.axis_index("dp")
    me = lax.axis_index("seq")
    my_x = me // n_z
    my_z = me % n_z
    my_quad = my_z // QUAD
    my_piece = my_x * QUAD + my_z % QUAD
    shard = gs.shape[1]

    def member(quad, piece):
        return (piece // QUAD) * n_z + quad * QUAD + piece % QUAD

    def piece_of(device):
        return (device // n_z) * QUAD + (device % n_z) % QUAD

    barrier = pltpu.get_barrier_semaphore()

    @pl.loop(1, n_seq)
    def _(step):
        pl.semaphore_signal(
            barrier, inc=1, device_id=(my_dp, (me + step) % n_seq), device_id_type=MESH
        )

    @pl.loop(1, n_dp)
    def _(step):
        pl.semaphore_signal(
            barrier, inc=1, device_id=((my_dp + step) % n_dp, me), device_id_type=MESH
        )

    loads = [
        pltpu.make_async_copy(source, target, load_sem.at[index])
        for index, (source, target) in enumerate(
            ((ld_hbm, ld), (k_hbm.at[0], k), (v_hbm.at[0], v), (q_hbm.at[0], q), (dy_hbm.at[0], dy))
        )
    ]
    for load in loads:
        load.start()

    loads[0].wait()
    lane_row = lax.broadcasted_iota(jnp.int32, (LANES, LANES), 0)
    lane_col = lax.broadcasted_iota(jnp.int32, (LANES, LANES), 1)
    upper = jnp.where(lane_row <= lane_col, 1.0, 0.0).astype(F32)
    log_rows = ld[...]
    within = jnp.dot(log_rows, upper, precision=EXACT, preferred_element_type=F32)
    totals = jnp.dot(
        log_rows, jnp.ones((LANES, LANES), F32), precision=EXACT, preferred_element_type=F32
    )
    chunk_row = lax.broadcasted_iota(jnp.int32, (chunks, LANES), 0)
    before = jnp.zeros((chunks, LANES), F32)
    for chunk in range(chunks - 1):
        before = before + jnp.where(chunk_row > chunk, totals[chunk : chunk + 1, :], 0.0)
    cum8 = within + before
    whole = before[chunks - 1 : chunks, :] + totals[chunks - 1 : chunks, :]
    own_log[...] = whole
    turned = cum8.T
    for chunk in range(chunks):
        span = pl.ds(chunk * LANES, LANES)
        wide = jnp.broadcast_to(turned[:, chunk : chunk + 1], (LANES, LANES))
        col[span, :] = wide
        tail[span, :] = jnp.exp(jnp.minimum(whole - wide, 0.0))

    loads[1].wait()
    loads[2].wait()
    keyed[...] = (k[...].astype(F32) * tail[...]).astype(BF16)
    local_state = dot(keyed[...], v[...], 0, 0)
    for piece in range(PIECES):
        state[piece] = local_state[piece * 16 : (piece + 1) * 16, :].astype(BF16)

    pl.semaphore_wait(barrier, n_seq - 1 + n_dp - 1)

    def spread(step, other_x):
        offset = jnp.where(step % 2 == 1, half - (step + 1) // 2, half + step // 2)
        target_x = (my_x + other_x) % X_PARTS
        return target_x * n_z + (my_z + offset) % n_z

    def to_owners(source, target, send, recv, with_log):
        def one(step, other_x):
            device = spread(step, other_x)
            if with_log:
                pltpu.make_async_remote_copy(
                    own_log, logs.at[me], log_send, log_recv,
                    device_id=(my_dp, device), device_id_type=MESH,
                ).start()
            pltpu.make_async_remote_copy(
                source.at[piece_of(device)], target.at[me], send, recv,
                device_id=(my_dp, device), device_id_type=MESH,
            ).start()

        @pl.loop(0, n_z - 1)
        def _(step):
            one(step, 1)
            one(step, 0)

        one(n_z - 1, 1)
        if with_log:
            pltpu.make_async_copy(own_log, logs.at[me], log_recv).start()
        pltpu.make_async_copy(source.at[my_piece], target.at[me], recv).start()

    def to_members(source, target, send, recv):
        @pl.loop(1, PIECES)
        def _(step):
            device = member(my_quad, (my_piece + step) % PIECES)
            pltpu.make_async_remote_copy(
                source.at[device], target.at[my_piece], send, recv,
                device_id=(my_dp, device), device_id_type=MESH,
            ).start()

        pltpu.make_async_copy(source.at[me], target.at[my_piece], recv).start()

    to_owners(state, gathered, s1_send, s1_recv, True)

    def columns(device):
        return pl.ds(pl.multiple_of(device * shard, LANES), shard)

    @pl.loop(1, n_dp)
    def _(step):
        device = (my_dp + step) % n_dp
        pltpu.make_async_remote_copy(
            pg_hbm.at[0, :, columns(device)], parts.at[my_dp], part_send, part_recv,
            device_id=(device, me), device_id_type=MESH,
        ).start()

    pltpu.make_async_copy(pg_hbm.at[0, :, columns(my_dp)], parts.at[my_dp], part_recv).start()

    loads[3].wait()
    loads[4].wait()
    lead[...] = jnp.exp(col[...])
    keyed[...] = (q[...].astype(F32) * lead[...]).astype(BF16)
    for block in range(blocks):
        rows = pl.ds(block * ROWS, ROWS)
        col_block = col[rows, :]
        for chunk in range((block + 1) * ROWS // LANES):
            at = pl.ds(chunk * LANES, LANES)
            weights = jnp.exp(jnp.minimum(col_block - cum8[chunk : chunk + 1, :], 0.0))
            if (chunk + 1) * LANES > block * ROWS:
                row_id = lax.broadcasted_iota(jnp.int32, (ROWS, LANES), 0) + block * ROWS
                col_id = lax.broadcasted_iota(jnp.int32, (ROWS, LANES), 1) + chunk * LANES
                weights = jnp.where(row_id >= col_id, weights, 0.0)
            mask[rows, at] = weights
        seen = (block + 1) * ROWS
        scores[rows, :seen] = (dot(q[rows, :], k[:seen, :], 1, 1) * mask[rows, :seen]).astype(BF16)
        attn[rows, :] = dot(scores[rows, :seen], v[:seen, :])

    def scan(order, source, target):
        decays = [jnp.exp(logs[device]) for device in range(n_seq)]
        total = jnp.zeros(source.shape[1:], F32)
        for device in order:
            target[device] = total.astype(BF16)
            total = total * decays[device] + source[device].astype(F32)

    wait_bytes(logs, log_recv)
    wait_bytes(gathered, s1_recv)
    scan(range(n_seq), gathered, prefix)
    to_members(prefix, incoming, s2_send, s2_recv)
    wait_bytes(incoming, s2_recv)

    start_state = incoming[...].reshape(width, width)
    for block in range(blocks):
        rows = pl.ds(block * ROWS, ROWS)
        full = attn[rows, :] + lead[rows, :] * dot(q[rows, :], start_state)
        square = jnp.sum(full * full, axis=1, keepdims=True) * (1.0 / width)
        ratio = lax.rsqrt(square + NORM_EPS)
        cotangent = dy[rows, :].astype(F32)
        along = jnp.sum(cotangent * full, axis=1, keepdims=True)
        normed = full * ratio
        out[rows, :] = normed.astype(BF16)
        dattn[rows, :] = (
            ratio * cotangent - (ratio * ratio * along * (1.0 / width)) * normed
        ).astype(BF16)

    local_future = dot(keyed[...], dattn[...], 0, 0)
    for piece in range(PIECES):
        state2[piece] = local_future[piece * 16 : (piece + 1) * 16, :].astype(BF16)
    to_owners(state2, gathered2, r1_send, r1_recv, False)
    out_store = pltpu.make_async_copy(out, out_hbm.at[0], store_sem.at[0])
    out_store.start()

    for block in range(blocks):
        rows = pl.ds(block * ROWS, ROWS)
        seen = (block + 1) * ROWS
        dscores = (dot(dattn[rows, :], v[:seen, :], 1, 1) * mask[rows, :seen]).astype(BF16)
        gq[rows, :] = (
            dot(dscores, k[:seen, :]) + lead[rows, :] * dot(dattn[rows, :], start_state, 1, 1)
        ).astype(BF16)
        key_part = dot(dscores, q[rows, :], 0, 0)
        value_part = dot(scores[rows, :seen], dattn[rows, :], 0, 0)
        old = block * ROWS
        if block:
            gkl[:old, :] = gkl[:old, :] + key_part[:old, :]
            gvl[:old, :] = gvl[:old, :] + value_part[:old, :]
        gkl[rows, :] = key_part[old:, :]
        gvl[rows, :] = value_part[old:, :]
    gq_store = pltpu.make_async_copy(gq, gq_hbm.at[0], store_sem.at[1])
    gq_store.start()

    wait_bytes(gathered2, r1_recv)
    scan(range(n_seq - 1, -1, -1), gathered2, prefix2)
    to_members(prefix2, outgoing, r2_send, r2_recv)

    wait_bytes(parts, part_recv)
    summed = parts[0].astype(F32)
    for device in range(1, n_dp):
        summed = summed + parts[device].astype(F32)
    gs[...] = summed
    gs_store = pltpu.make_async_copy(gs, gs_hbm, store_sem.at[2])
    gs_store.start()

    wait_bytes(outgoing, r2_recv)
    later = outgoing[...].reshape(width, width)
    stores = [out_store, gq_store, gs_store]
    for block in range(blocks):
        rows = pl.ds(block * ROWS, ROWS)
        fade = tail[rows, :]
        gk[rows, :] = (gkl[rows, :] + fade * dot(v[rows, :], later, 1, 1)).astype(BF16)
        gv[rows, :] = (gvl[rows, :] + fade * dot(k[rows, :], later)).astype(BF16)
    for index, (source, target) in enumerate(((gk, gk_hbm), (gv, gv_hbm))):
        store = pltpu.make_async_copy(source, target.at[0], store_sem.at[3 + index])
        store.start()
        stores.append(store)

    others = n_seq - 1
    wait_bytes(logs.at[pl.ds(0, others)], log_send)
    wait_bytes(gathered.at[pl.ds(0, others)], s1_send)
    wait_bytes(gathered2.at[pl.ds(0, others)], r1_send)
    wait_bytes(incoming.at[pl.ds(0, PIECES - 1)], s2_send)
    wait_bytes(outgoing.at[pl.ds(0, PIECES - 1)], r2_send)
    wait_bytes(parts.at[pl.ds(0, n_dp - 1)], part_send)
    for store in stores:
        store.wait()


def local(n_dp, n_seq, queries, key_vectors, value_vectors, out_grad, log_decay, prev_grads):
    tokens, width = queries.shape[1:]
    grad_rows, grad_cols = prev_grads.shape[1:]
    shard = grad_cols // n_dp
    chunks = tokens // LANES
    wide = jax.ShapeDtypeStruct((1, tokens, width), BF16)
    rows16 = pltpu.VMEM((tokens, width), BF16)
    rows32 = pltpu.VMEM((tokens, width), F32)
    pieces = pltpu.VMEM((PIECES, width // PIECES, width), BF16)
    gather = pltpu.VMEM((n_seq, width // PIECES, width), BF16)
    dma = pltpu.SemaphoreType.DMA
    outs = pl.pallas_call(
        functools.partial(kernel, n_dp, n_seq),
        out_shape=(wide, wide, wide, wide, jax.ShapeDtypeStruct((grad_rows, shard), F32)),
        in_specs=[pl.BlockSpec(memory_space=pl.ANY)] * 6,
        out_specs=[pl.BlockSpec(memory_space=pl.ANY)] * 5,
        scratch_shapes=[
            rows16, rows16, rows16, rows16,
            pltpu.VMEM((chunks, LANES), F32),
            rows16, rows16, rows16, rows16,
            pltpu.VMEM((grad_rows, shard), F32),
            rows32, rows32, rows32,
            pltpu.VMEM((tokens, tokens), F32),
            pltpu.VMEM((tokens, tokens), BF16),
            rows16, rows32, rows16, rows32, rows32,
            pieces, gather, gather, pieces, pieces, gather, gather, pieces,
            pltpu.VMEM((1, LANES), F32),
            pltpu.VMEM((n_seq, 1, LANES), F32),
            pltpu.VMEM((n_dp, grad_rows, shard), BF16),
            dma((5,)), dma((5,)),
        ]
        + [dma(())] * 5
        + [dma(())] * 8,
        compiler_params=pltpu.CompilerParams(collective_id=0, has_side_effects=True),
        name="attention",
    )(
        queries, key_vectors, value_vectors, out_grad,
        log_decay.reshape(chunks, LANES), prev_grads,
    )
    return tuple(outs)


def solution(mesh):
    return jax.shard_map(
        functools.partial(local, mesh.shape["dp"], mesh.shape["seq"]),
        mesh=mesh,
        in_specs=(
            P("dp", "seq", None),
            P("dp", "seq", None),
            P("dp", "seq", None),
            P("dp", "seq", None),
            P("dp", None, "seq"),
            P("dp", "seq", None),
        ),
        out_specs=(
            P("dp", "seq", None),
            P("dp", "seq", None),
            P("dp", "seq", None),
            P("dp", "seq", None),
            P("seq", "dp"),
        ),
        check_vma=False,
    )
```

time: 326 us -> 49.6 us (0.15)
  waiting for transfers between devices: 167 us -> 0 us
  blocking collectives: 69.9 us -> 0 us
  Pallas kernels: 0 us -> 43.3 us
  matrix products: 26.8 us -> 0 us
  local copies, waits for them, and re-layouts: 27.9 us -> 5.22 us
  between operations: 17.1 us -> 0.65 us
  other arithmetic: 9.85 us -> 0 us
  loops' own time: 5.81 us -> 0 us
    all_gather x2 -> x0, waiting for transfers between devices: 167 us -> none  [the longest x1 120 us: local(): lax.all_gather(local_future[None].astype(jnp.bfloat16), 'seq', axis=0, ti...]
    unnamed x1 -> x0, blocking collectives: 69.9 us -> none
    pallas_call x0 -> x1, Pallas kernels: none -> 43.3 us  [local(): pl.pallas_call(functools.partial(kernel, n_dp, n_seq), out_shape=(wide, w...]
    dot_general x32 -> x0, matrix products: 26.8 us -> none  [the longest x22 16.3 us: product(): jnp.dot(left, right, precision=FULL_PRECISION, preferred_element_type=jnp...]
    unnamed x36 -> x13, local copies, waits for them, and re-layouts: 15.1 us -> 5.22 us
    slice x12 -> x0, local copies, waits for them, and re-layouts: 6.21 us -> none  [the longest x4 2.34 us: advance(): running[-1]]
    another operation x2 -> x0, loops' own time: 5.81 us -> none  [the longest x1 2.92 us: backward_local(): lax.scan(retreat, jnp.zeros((head_width, head_width), jnp.float32), (quer...]
    another operation x11 -> x0, other arithmetic: 3.48 us -> none
  transfers between devices with their start and end apart: 3 -> 0, of which waited for: 2 -> 0; matrix products, arithmetic and copies ran while one was open for 14% -> 0% of each run, Pallas kernels for 0% -> 0%
where the time goes in v1:
time: 49.6 us; the launch traced here: 49.1 us
  Pallas kernels  43.3 us (87%)
  local copies, waits for them, and re-layouts  5.22 us (11%)
  between operations  0.65 us (1%)
    pallas_call x1, Pallas kernels, local(): pl.pallas_call(functools.partial(kernel, n_dp, n_seq), out_shape=(wide, w...  43.3 us
    unnamed x13, local copies, waits for them, and re-layouts  5.22 us

profile of v1, /device:TPU:6, one launch (start us, length us, event | category | flops | bytes accessed | tf_op | source)
XLA Modules:
  0.0 49.1 jit_solution(5776560886781648211)
XLA Ops:
  0.6 43.3 %attention.1 = (bf16[1,1024,128]{2,1,0:T(8,128)(2,1)}, bf16[1,1024,128]{2,1,0:T(8,128)(2,1)}, bf16[1,1024,128]{2,1,0:T(8,128)(2,1)}, bf16[1,1024,128]{2,1,0:T(8,128)(2,1)}, f32[32,384]{1,0:T(8,128)}) custom-call(bf16[1,1024,128]{2,1,0:T(8,128)(2,1)} %q_hbm.1, bf16[1,1024,128]{2,1,0:T(8,128)(2,1)} %k_hbm.1, bf16[1,1024,128]{2,1,0:T(8,128)(2,1)} %v_hbm.1, ...), custom_call_target="tpu_custom_call" | custom-call | tf_op jit(solution)/shard_map/attention/pallas_call | solution.py:290
  43.9 0.0 copy-start.2
  43.9 1.7 %copy.16 = bf16[1,1024,128]{2,1,0:T(8,128)(2,1)} copy(bf16[1,1024,128]{2,1,0:T(8,128)(2,1)} %get-tuple-element.10) | data formatting | bytes 524288
  45.6 0.0 copy-done.2
  45.6 0.0 copy-start.1
  45.6 0.7 %copy.17 = bf16[1,1024,128]{2,1,0:T(8,128)(2,1)} copy(bf16[1,1024,128]{2,1,0:T(8,128)(2,1)S(1)} %copy-done.2) | data formatting | bytes 524288
  46.3 0.3 copy-done.1
  46.7 0.0 copy-start
  46.7 0.7 %copy.18 = bf16[1,1024,128]{2,1,0:T(8,128)(2,1)} copy(bf16[1,1024,128]{2,1,0:T(8,128)(2,1)S(1)} %copy-done.1) | data formatting | bytes 524288
  47.4 0.3 copy-done
  47.7 0.0 copy-start.3
  47.7 0.7 %copy.19 = bf16[1,1024,128]{2,1,0:T(8,128)(2,1)} copy(bf16[1,1024,128]{2,1,0:T(8,128)(2,1)S(1)} %copy-done) | data formatting | bytes 524288
  48.4 0.1 copy-done.3
  48.5 0.6 %copy.20 = f32[32,384]{1,0:T(8,128)} copy(f32[32,384]{1,0:T(8,128)S(1)} %copy-done.3) | data formatting | bytes 98304
Async XLA Ops:
  43.9 1.7 %copy-start.2 = (bf16[1,1024,128]{2,1,0:T(8,128)(2,1)S(1)}, bf16[1,1024,128]{2,1,0:T(8,128)(2,1)}, u32[]{:S(2)}) copy-start(bf16[1,1024,128]{2,1,0:T(8,128)(2,1)} %get-tuple-element.11) | copy-start | bytes 786436
  45.6 1.0 %copy-start.1 = (bf16[1,1024,128]{2,1,0:T(8,128)(2,1)S(1)}, bf16[1,1024,128]{2,1,0:T(8,128)(2,1)}, u32[]{:S(2)}) copy-start(bf16[1,1024,128]{2,1,0:T(8,128)(2,1)} %get-tuple-element.12) | copy-start | bytes 786436
  46.7 1.0 %copy-start = (bf16[1,1024,128]{2,1,0:T(8,128)(2,1)S(1)}, bf16[1,1024,128]{2,1,0:T(8,128)(2,1)}, u32[]{:S(2)}) copy-start(bf16[1,1024,128]{2,1,0:T(8,128)(2,1)} %get-tuple-element.13) | copy-start | bytes 786436
  47.7 0.8 %copy-start.3 = (f32[32,384]{1,0:T(8,128)S(1)}, f32[32,384]{1,0:T(8,128)}, u32[]{:S(2)}) copy-start(f32[32,384]{1,0:T(8,128)} %get-tuple-element.14) | copy-start | bytes 147460

commit v2 on v1

--- a/solution.py
+++ b/solution.py
@@ -33,12 +33,11 @@
 def kernel(
     n_dp, n_seq,
     q_hbm, k_hbm, v_hbm, dy_hbm, ld_hbm, pg_hbm,
-    out_hbm, gq_hbm, gk_hbm, gv_hbm, gs_hbm,
-    q, k, v, dy, ld, out, gq, gk, gv, gs,
-    col, lead, tail, mask, scores, keyed, attn, dattn, gkl, gvl,
-    state, gathered, prefix, incoming, state2, gathered2, prefix2, outgoing,
+    k, v, tail, gkl, gvl, outgoing, out, gq, gs,
+    q, dy, ld, col, lead, mask, scores, keyed, attn, dattn,
+    state, gathered, prefix, incoming, state2, gathered2, prefix2,
     own_log, logs, parts,
-    load_sem, store_sem, part_send, part_recv, log_send, log_recv, own_sem,
+    load_sem, part_send, part_recv, log_send, log_recv,
     s1_send, s1_recv, s2_send, s2_recv, r1_send, r1_recv, r2_send, r2_recv,
 ):
     tokens, width = q.shape
@@ -57,21 +56,35 @@
     def member(quad, piece):
         return (piece // QUAD) * n_z + quad * QUAD + piece % QUAD
 
-    def piece_of(device):
-        return (device // n_z) * QUAD + (device % n_z) % QUAD
-
     barrier = pltpu.get_barrier_semaphore()
 
-    @pl.loop(1, n_seq)
-    def _(step):
+    def each_far_first(one):
+        other_x = X_PARTS - 1 - my_x
+
+        def pair(z):
+            one(other_x, z)
+            one(my_x, z)
+
+        pair(lax.rem(my_z + half, n_z))
+
+        @pl.loop(1, half)
+        def _(step):
+            pair(lax.rem(my_z + half - step, n_z))
+            pair(lax.rem(my_z + half + step, n_z))
+
+        one(other_x, my_z)
+
+    def greet(x, z):
         pl.semaphore_signal(
-            barrier, inc=1, device_id=(my_dp, (me + step) % n_seq), device_id_type=MESH
+            barrier, inc=1, device_id=(my_dp, x * n_z + z), device_id_type=MESH
         )
+
+    each_far_first(greet)
 
     @pl.loop(1, n_dp)
     def _(step):
         pl.semaphore_signal(
-            barrier, inc=1, device_id=((my_dp + step) % n_dp, me), device_id_type=MESH
+            barrier, inc=1, device_id=(lax.rem(my_dp + step, n_dp), me), device_id_type=MESH
         )
 
     loads = [
@@ -115,38 +128,64 @@
 
     pl.semaphore_wait(barrier, n_seq - 1 + n_dp - 1)
 
-    def spread(step, other_x):
-        offset = jnp.where(step % 2 == 1, half - (step + 1) // 2, half + step // 2)
-        target_x = (my_x + other_x) % X_PARTS
-        return target_x * n_z + (my_z + offset) % n_z
-
-    def to_owners(source, target, send, recv, with_log):
-        def one(step, other_x):
-            device = spread(step, other_x)
-            if with_log:
+    quads = n_z // QUAD
+
+    def to_owners(source, target, send, recv, forward):
+        free = my_x == (0 if forward else X_PARTS - 1)
+        slot = jnp.where(free, 0, my_quad + 1)
+
+        def one(x, z):
+            device = (my_dp, x * n_z + z)
+            quad = z // QUAD
+            if forward:
                 pltpu.make_async_remote_copy(
                     own_log, logs.at[me], log_send, log_recv,
-                    device_id=(my_dp, device), device_id_type=MESH,
+                    device_id=device, device_id_type=MESH,
                 ).start()
-            pltpu.make_async_remote_copy(
-                source.at[piece_of(device)], target.at[me], send, recv,
-                device_id=(my_dp, device), device_id_type=MESH,
-            ).start()
-
-        @pl.loop(0, n_z - 1)
-        def _(step):
-            one(step, 1)
-            one(step, 0)
-
-        one(n_z - 1, 1)
-        if with_log:
+            needed = quad >= my_quad if forward else quad <= my_quad
+
+            @pl.when(free | needed)
+            def _():
+                pltpu.make_async_remote_copy(
+                    source.at[x * QUAD + lax.rem(z, QUAD)], target.at[me],
+                    send.at[quad], recv.at[slot],
+                    device_id=device, device_id_type=MESH,
+                ).start()
+
+        each_far_first(one)
+        if forward:
             pltpu.make_async_copy(own_log, logs.at[me], log_recv).start()
-        pltpu.make_async_copy(source.at[my_piece], target.at[me], recv).start()
+        pltpu.make_async_copy(source.at[my_piece], target.at[me], recv.at[slot]).start()
+
+    def owners_sent(target, send, forward):
+        free = my_x == (0 if forward else X_PARTS - 1)
+        for quad in range(quads):
+            needed = my_quad <= quad if forward else my_quad >= quad
+
+            @pl.when((free | needed) & (my_quad != quad))
+            def _():
+                wait_bytes(target.at[pl.ds(0, PIECES)], send.at[quad])
+
+            @pl.when(my_quad == quad)
+            def _():
+                wait_bytes(target.at[pl.ds(0, PIECES - 1)], send.at[quad])
+
+    def owners_received(target, recv, forward):
+        free = 0 if forward else X_PARTS - 1
+        wait_bytes(target.at[pl.ds(free * n_z, n_z)], recv.at[0])
+        for quad in range(quads):
+
+            @pl.when(my_quad >= quad if forward else my_quad <= quad)
+            def _():
+                wait_bytes(
+                    target.at[pl.ds((X_PARTS - 1 - free) * n_z + quad * QUAD, QUAD)],
+                    recv.at[quad + 1],
+                )
 
     def to_members(source, target, send, recv):
         @pl.loop(1, PIECES)
         def _(step):
-            device = member(my_quad, (my_piece + step) % PIECES)
+            device = member(my_quad, lax.rem(my_piece + step, PIECES))
             pltpu.make_async_remote_copy(
                 source.at[device], target.at[my_piece], send, recv,
                 device_id=(my_dp, device), device_id_type=MESH,
@@ -161,7 +200,7 @@
 
     @pl.loop(1, n_dp)
     def _(step):
-        device = (my_dp + step) % n_dp
+        device = lax.rem(my_dp + step, n_dp)
         pltpu.make_async_remote_copy(
             pg_hbm.at[0, :, columns(device)], parts.at[my_dp], part_send, part_recv,
             device_id=(device, me), device_id_type=MESH,
@@ -196,7 +235,7 @@
             total = total * decays[device] + source[device].astype(F32)
 
     wait_bytes(logs, log_recv)
-    wait_bytes(gathered, s1_recv)
+    owners_received(gathered, s1_recv, True)
     scan(range(n_seq), gathered, prefix)
     to_members(prefix, incoming, s2_send, s2_recv)
     wait_bytes(incoming, s2_recv)
@@ -219,8 +258,6 @@
     for piece in range(PIECES):
         state2[piece] = local_future[piece * 16 : (piece + 1) * 16, :].astype(BF16)
     to_owners(state2, gathered2, r1_send, r1_recv, False)
-    out_store = pltpu.make_async_copy(out, out_hbm.at[0], store_sem.at[0])
-    out_store.start()
 
     for block in range(blocks):
         rows = pl.ds(block * ROWS, ROWS)
@@ -237,10 +274,8 @@
             gvl[:old, :] = gvl[:old, :] + value_part[:old, :]
         gkl[rows, :] = key_part[old:, :]
         gvl[rows, :] = value_part[old:, :]
-    gq_store = pltpu.make_async_copy(gq, gq_hbm.at[0], store_sem.at[1])
-    gq_store.start()
-
-    wait_bytes(gathered2, r1_recv)
+
+    owners_received(gathered2, r1_recv, False)
     scan(range(n_seq - 1, -1, -1), gathered2, prefix2)
     to_members(prefix2, outgoing, r2_send, r2_recv)
 
@@ -249,29 +284,45 @@
     for device in range(1, n_dp):
         summed = summed + parts[device].astype(F32)
     gs[...] = summed
-    gs_store = pltpu.make_async_copy(gs, gs_hbm, store_sem.at[2])
-    gs_store.start()
 
     wait_bytes(outgoing, r2_recv)
+
+    others = n_seq - 1
+    wait_bytes(logs.at[pl.ds(0, others)], log_send)
+    owners_sent(gathered, s1_send, True)
+    owners_sent(gathered2, r1_send, False)
+    wait_bytes(incoming.at[pl.ds(0, PIECES - 1)], s2_send)
+    wait_bytes(outgoing.at[pl.ds(0, PIECES - 1)], r2_send)
+    wait_bytes(parts.at[pl.ds(0, n_dp - 1)], part_send)
+
+
+def finish(
+    k, v, tail, gkl, gvl, outgoing, out, gq, gs,
+    out_hbm, gq_hbm, gk_hbm, gv_hbm, gs_hbm,
+    gk, gv, early_sem, late_sem,
+):
+    tokens, width = k.shape
+    blocks = tokens // ROWS
+    stores = [
+        pltpu.make_async_copy(source, target, early_sem.at[index])
+        for index, (source, target) in enumerate(
+            ((out, out_hbm.at[0]), (gq, gq_hbm.at[0]), (gs, gs_hbm))
+        )
+    ]
+    for store in stores:
+        store.start()
     later = outgoing[...].reshape(width, width)
-    stores = [out_store, gq_store, gs_store]
     for block in range(blocks):
         rows = pl.ds(block * ROWS, ROWS)
         fade = tail[rows, :]
         gk[rows, :] = (gkl[rows, :] + fade * dot(v[rows, :], later, 1, 1)).astype(BF16)
         gv[rows, :] = (gvl[rows, :] + fade * dot(k[rows, :], later)).astype(BF16)
-    for index, (source, target) in enumerate(((gk, gk_hbm), (gv, gv_hbm))):
-        store = pltpu.make_async_copy(source, target.at[0], store_sem.at[3 + index])
-        store.start()
-        stores.append(store)
-
-    others = n_seq - 1
-    wait_bytes(logs.at[pl.ds(0, others)], log_send)
-    wait_bytes(gathered.at[pl.ds(0, others)], s1_send)
-    wait_bytes(gathered2.at[pl.ds(0, others)], r1_send)
-    wait_bytes(incoming.at[pl.ds(0, PIECES - 1)], s2_send)
-    wait_bytes(outgoing.at[pl.ds(0, PIECES - 1)], r2_send)
-    wait_bytes(parts.at[pl.ds(0, n_dp - 1)], part_send)
+        for index, (source, target) in enumerate(((gk, gk_hbm), (gv, gv_hbm))):
+            store = pltpu.make_async_copy(
+                source.at[rows], target.at[0, rows], late_sem.at[2 * block + index]
+            )
+            store.start()
+            stores.append(store)
     for store in stores:
         store.wait()
 
@@ -281,40 +332,59 @@
     grad_rows, grad_cols = prev_grads.shape[1:]
     shard = grad_cols // n_dp
     chunks = tokens // LANES
+    quads = n_seq // PIECES
     wide = jax.ShapeDtypeStruct((1, tokens, width), BF16)
     rows16 = pltpu.VMEM((tokens, width), BF16)
     rows32 = pltpu.VMEM((tokens, width), F32)
     pieces = pltpu.VMEM((PIECES, width // PIECES, width), BF16)
     gather = pltpu.VMEM((n_seq, width // PIECES, width), BF16)
     dma = pltpu.SemaphoreType.DMA
-    outs = pl.pallas_call(
+    held = (
+        rows16, rows16, rows32, rows32, rows32, pieces, rows16, rows16,
+        pltpu.VMEM((grad_rows, shard), F32),
+    )
+    middle = pl.pallas_call(
         functools.partial(kernel, n_dp, n_seq),
-        out_shape=(wide, wide, wide, wide, jax.ShapeDtypeStruct((grad_rows, shard), F32)),
-        in_specs=[pl.BlockSpec(memory_space=pl.ANY)] * 6,
-        out_specs=[pl.BlockSpec(memory_space=pl.ANY)] * 5,
+        out_shape=held,
+        in_specs=[pl.BlockSpec(memory_space=pltpu.HBM)] * 6,
+        out_specs=[pl.BlockSpec(memory_space=pltpu.VMEM)] * len(held),
         scratch_shapes=[
-            rows16, rows16, rows16, rows16,
+            rows16, rows16,
             pltpu.VMEM((chunks, LANES), F32),
-            rows16, rows16, rows16, rows16,
-            pltpu.VMEM((grad_rows, shard), F32),
-            rows32, rows32, rows32,
+            rows32, rows32,
             pltpu.VMEM((tokens, tokens), F32),
             pltpu.VMEM((tokens, tokens), BF16),
-            rows16, rows32, rows16, rows32, rows32,
-            pieces, gather, gather, pieces, pieces, gather, gather, pieces,
+            rows16, rows32, rows16,
+            pieces, gather, gather, pieces, pieces, gather, gather,
             pltpu.VMEM((1, LANES), F32),
             pltpu.VMEM((n_seq, 1, LANES), F32),
             pltpu.VMEM((n_dp, grad_rows, shard), BF16),
-            dma((5,)), dma((5,)),
+            dma((5,)),
         ]
-        + [dma(())] * 5
-        + [dma(())] * 8,
-        compiler_params=pltpu.CompilerParams(collective_id=0, has_side_effects=True),
+        + [dma(())] * 4
+        + [dma((quads,)), dma((quads + 1,)), dma(()), dma(())] * 2,
+        compiler_params=pltpu.CompilerParams(
+            collective_id=0, has_side_effects=True, vmem_limit_bytes=32 * 1024 * 1024
+        ),
         name="attention",
     )(
-        queries, key_vectors, value_vectors, out_grad,
-        log_decay.reshape(chunks, LANES), prev_grads,
+        *(
+            pltpu.with_memory_space_constraint(array, pltpu.HBM)
+            for array in (
+                queries, key_vectors, value_vectors, out_grad,
+                log_decay.reshape(chunks, LANES), prev_grads,
+            )
+        )
     )
+    outs = pl.pallas_call(
+        finish,
+        out_shape=(wide, wide, wide, wide, jax.ShapeDtypeStruct((grad_rows, shard), F32)),
+        in_specs=[pl.BlockSpec(memory_space=pltpu.VMEM)] * len(held),
+        out_specs=[pl.BlockSpec(memory_space=pl.ANY)] * 5,
+        scratch_shapes=[rows16, rows16, dma((3,)), dma((2 * (tokens // ROWS),))],
+        compiler_params=pltpu.CompilerParams(vmem_limit_bytes=8 * 1024 * 1024),
+        name="finish",
+    )(*middle)
     return tuple(outs)
 
 

time: 49.6 us -> 44.3 us (0.89)
  local copies, waits for them, and re-layouts: 5.22 us -> 0 us
    unnamed x13 -> x0, local copies, waits for them, and re-layouts: 5.22 us -> none
    pallas_call x1 -> x2, Pallas kernels: 43.3 us -> 43.5 us  [the longest x1 42.4 us: local(): pl.pallas_call(functools.partial(kernel, n_dp, n_seq), out_shape=held, in...]
where the time goes in v2:
time: 44.3 us; the launch traced here: 44.1 us
  Pallas kernels  43.5 us (98%)
  between operations  0.64 us (1%)
    pallas_call x1, Pallas kernels, local(): pl.pallas_call(functools.partial(kernel, n_dp, n_seq), out_shape=held, in...  42.4 us
    pallas_call x1, Pallas kernels, local(): pl.pallas_call(finish, out_shape=(wide, wide, wide, wide, jax.ShapeDtypeS...  1.07 us

profile of v2, /device:TPU:6, one launch (start us, length us, event | category | flops | bytes accessed | tf_op | source)
XLA Modules:
  0.0 44.1 jit_solution(15016285719096376990)
XLA Ops:
  0.6 42.4 %attention.1 = (bf16[1024,128]{1,0:T(8,128)(2,1)S(1)}, bf16[1024,128]{1,0:T(8,128)(2,1)S(1)}, f32[1024,128]{1,0:T(8,128)S(1)}, f32[1024,128]{1,0:T(8,128)S(1)}, ...) custom-call(bf16[1,1024,128]{2,1,0:T(8,128)(2,1)} %q_hbm.1, ...), custom_call_target="tpu_custom_call" | custom-call | tf_op jit(solution)/shard_map/attention/pallas_call | solution.py:346
  43.0 1.1 %finish.1 = (bf16[1,1024,128]{2,1,0:T(8,128)(2,1)}, bf16[1,1024,128]{2,1,0:T(8,128)(2,1)}, bf16[1,1024,128]{2,1,0:T(8,128)(2,1)}, bf16[1,1024,128]{2,1,0:T(8,128)(2,1)}, f32[32,384]{1,0:T(8,128)}) custom-call(bf16[1024,128]{1,0:T(8,128)(2,1)S(1)} %get-tuple-element.14.k, bf16[1024,128]{1,0:T(8,128)(2,1)S(1)} %get-tuple-element.15.v, ...), custom_call_target="tpu_custom_call" | custom-call | tf_op jit(solution)/shard_map/finish/pallas_call | solution.py:379

commit v3 on v2

--- a/solution.py
+++ b/solution.py
@@ -46,6 +46,9 @@
     n_z = n_seq // X_PARTS
     half = n_z // 2
     my_dp = lax.axis_index("dp")
+    side = lax.rem(my_dp, 2)
+    owning = side == 1
+    owner_dp = my_dp + 1 - side
     me = lax.axis_index("seq")
     my_x = me // n_z
     my_z = me % n_z
@@ -74,12 +77,23 @@
 
         one(other_x, my_z)
 
-    def greet(x, z):
-        pl.semaphore_signal(
-            barrier, inc=1, device_id=(my_dp, x * n_z + z), device_id_type=MESH
-        )
-
-    each_far_first(greet)
+    def greet(dp, device):
+        pl.semaphore_signal(barrier, inc=1, device_id=(dp, device), device_id_type=MESH)
+
+    @pl.when(owning)
+    def _():
+        def both(x, z):
+            greet(my_dp - 1, x * n_z + z)
+            greet(my_dp, x * n_z + z)
+
+        each_far_first(both)
+        greet(my_dp - 1, me)
+
+    @pl.when(jnp.logical_not(owning))
+    def _():
+        @pl.loop(0, PIECES)
+        def _(piece):
+            greet(owner_dp, member(my_quad, piece))
 
     @pl.loop(1, n_dp)
     def _(step):
@@ -126,7 +140,7 @@
     for piece in range(PIECES):
         state[piece] = local_state[piece * 16 : (piece + 1) * 16, :].astype(BF16)
 
-    pl.semaphore_wait(barrier, n_seq - 1 + n_dp - 1)
+    pl.semaphore_wait(barrier, n_dp - 1 + jnp.where(owning, n_seq - 1 + PIECES, n_seq))
 
     quads = n_z // QUAD
 
@@ -135,11 +149,11 @@
         slot = jnp.where(free, 0, my_quad + 1)
 
         def one(x, z):
-            device = (my_dp, x * n_z + z)
+            device = (owner_dp, x * n_z + z)
             quad = z // QUAD
             if forward:
                 pltpu.make_async_remote_copy(
-                    own_log, logs.at[me], log_send, log_recv,
+                    own_log, logs.at[side, me], log_send, log_recv.at[side],
                     device_id=device, device_id_type=MESH,
                 ).start()
             needed = quad >= my_quad if forward else quad <= my_quad
@@ -147,28 +161,38 @@
             @pl.when(free | needed)
             def _():
                 pltpu.make_async_remote_copy(
-                    source.at[x * QUAD + lax.rem(z, QUAD)], target.at[me],
-                    send.at[quad], recv.at[slot],
+                    source.at[x * QUAD + lax.rem(z, QUAD)], target.at[side, me],
+                    send.at[quad], recv.at[side, slot],
                     device_id=device, device_id_type=MESH,
                 ).start()
 
         each_far_first(one)
-        if forward:
-            pltpu.make_async_copy(own_log, logs.at[me], log_recv).start()
-        pltpu.make_async_copy(source.at[my_piece], target.at[me], recv.at[slot]).start()
+
+        @pl.when(owning)
+        def _():
+            if forward:
+                pltpu.make_async_copy(own_log, logs.at[1, me], log_recv.at[1]).start()
+            pltpu.make_async_copy(
+                source.at[my_piece], target.at[1, me], recv.at[1, slot]
+            ).start()
+
+        @pl.when(jnp.logical_not(owning))
+        def _():
+            one(my_x, my_z)
 
     def owners_sent(target, send, forward):
         free = my_x == (0 if forward else X_PARTS - 1)
         for quad in range(quads):
             needed = my_quad <= quad if forward else my_quad >= quad
-
-            @pl.when((free | needed) & (my_quad != quad))
+            short = owning & (my_quad == quad)
+
+            @pl.when((free | needed) & jnp.logical_not(short))
             def _():
-                wait_bytes(target.at[pl.ds(0, PIECES)], send.at[quad])
-
-            @pl.when(my_quad == quad)
+                wait_bytes(target.at[0, pl.ds(0, PIECES)], send.at[quad])
+
+            @pl.when(short)
             def _():
-                wait_bytes(target.at[pl.ds(0, PIECES - 1)], send.at[quad])
+                wait_bytes(target.at[0, pl.ds(0, PIECES - 1)], send.at[quad])
 
     def owners_received(target, recv, forward):
         free = 0 if forward else X_PARTS - 1
@@ -182,16 +206,41 @@
                     recv.at[quad + 1],
                 )
 
-    def to_members(source, target, send, recv):
-        @pl.loop(1, PIECES)
-        def _(step):
-            device = member(my_quad, lax.rem(my_piece + step, PIECES))
-            pltpu.make_async_remote_copy(
-                source.at[device], target.at[my_piece], send, recv,
-                device_id=(my_dp, device), device_id_type=MESH,
-            ).start()
-
-        pltpu.make_async_copy(source.at[me], target.at[my_piece], recv).start()
+    def scan(order, decay_logs, source, target):
+        decays = [jnp.exp(decay_logs[device]) for device in range(n_seq)]
+        total = jnp.zeros(source.shape[1:], F32)
+        for device in order:
+            target[device] = total.astype(BF16)
+            total = total * decays[device] + source[device].astype(F32)
+
+    def serve(target, recv, pieces, result, member_send, member_recv, forward):
+        @pl.when(owning)
+        def _():
+            for core in (1, 0):
+                if forward:
+                    wait_bytes(logs.at[core], log_recv.at[core])
+                owners_received(target.at[core], recv.at[core], forward)
+                order = range(n_seq) if forward else range(n_seq - 1, -1, -1)
+                scan(order, logs.at[core], target.at[core], pieces.at[core])
+                dp = my_dp - 1 + core
+
+                @pl.loop(1, PIECES)
+                def _(step):
+                    device = member(my_quad, lax.rem(my_piece + step, PIECES))
+                    pltpu.make_async_remote_copy(
+                        pieces.at[core, device], result.at[my_piece], member_send, member_recv,
+                        device_id=(dp, device), device_id_type=MESH,
+                    ).start()
+
+                if core:
+                    pltpu.make_async_copy(
+                        pieces.at[core, me], result.at[my_piece], member_recv
+                    ).start()
+                else:
+                    pltpu.make_async_remote_copy(
+                        pieces.at[core, me], result.at[my_piece], member_send, member_recv,
+                        device_id=(dp, me), device_id_type=MESH,
+                    ).start()
 
     to_owners(state, gathered, s1_send, s1_recv, True)
 
@@ -227,17 +276,7 @@
         scores[rows, :seen] = (dot(q[rows, :], k[:seen, :], 1, 1) * mask[rows, :seen]).astype(BF16)
         attn[rows, :] = dot(scores[rows, :seen], v[:seen, :])
 
-    def scan(order, source, target):
-        decays = [jnp.exp(logs[device]) for device in range(n_seq)]
-        total = jnp.zeros(source.shape[1:], F32)
-        for device in order:
-            target[device] = total.astype(BF16)
-            total = total * decays[device] + source[device].astype(F32)
-
-    wait_bytes(logs, log_recv)
-    owners_received(gathered, s1_recv, True)
-    scan(range(n_seq), gathered, prefix)
-    to_members(prefix, incoming, s2_send, s2_recv)
+    serve(gathered, s1_recv, prefix, incoming, s2_send, s2_recv, True)
     wait_bytes(incoming, s2_recv)
 
     start_state = incoming[...].reshape(width, width)
@@ -275,9 +314,7 @@
         gkl[rows, :] = key_part[old:, :]
         gvl[rows, :] = value_part[old:, :]
 
-    owners_received(gathered2, r1_recv, False)
-    scan(range(n_seq - 1, -1, -1), gathered2, prefix2)
-    to_members(prefix2, outgoing, r2_send, r2_recv)
+    serve(gathered2, r1_recv, prefix2, outgoing, r2_send, r2_recv, False)
 
     wait_bytes(parts, part_recv)
     summed = parts[0].astype(F32)
@@ -287,12 +324,20 @@
 
     wait_bytes(outgoing, r2_recv)
 
-    others = n_seq - 1
-    wait_bytes(logs.at[pl.ds(0, others)], log_send)
     owners_sent(gathered, s1_send, True)
     owners_sent(gathered2, r1_send, False)
-    wait_bytes(incoming.at[pl.ds(0, PIECES - 1)], s2_send)
-    wait_bytes(outgoing.at[pl.ds(0, PIECES - 1)], r2_send)
+
+    @pl.when(owning)
+    def _():
+        wait_bytes(logs.at[0, pl.ds(0, n_seq - 1)], log_send)
+        sent = pl.ds(0, 2 * PIECES - 1)
+        wait_bytes(prefix.at[0, sent], s2_send)
+        wait_bytes(prefix2.at[0, sent], r2_send)
+
+    @pl.when(jnp.logical_not(owning))
+    def _():
+        wait_bytes(logs.at[0], log_send)
+
     wait_bytes(parts.at[pl.ds(0, n_dp - 1)], part_send)
 
 
@@ -337,7 +382,7 @@
     rows16 = pltpu.VMEM((tokens, width), BF16)
     rows32 = pltpu.VMEM((tokens, width), F32)
     pieces = pltpu.VMEM((PIECES, width // PIECES, width), BF16)
-    gather = pltpu.VMEM((n_seq, width // PIECES, width), BF16)
+    gather = pltpu.VMEM((2, n_seq, width // PIECES, width), BF16)
     dma = pltpu.SemaphoreType.DMA
     held = (
         rows16, rows16, rows32, rows32, rows32, pieces, rows16, rows16,
@@ -357,12 +402,13 @@
             rows16, rows32, rows16,
             pieces, gather, gather, pieces, pieces, gather, gather,
             pltpu.VMEM((1, LANES), F32),
-            pltpu.VMEM((n_seq, 1, LANES), F32),
+            pltpu.VMEM((2, n_seq, 1, LANES), F32),
             pltpu.VMEM((n_dp, grad_rows, shard), BF16),
             dma((5,)),
         ]
-        + [dma(())] * 4
-        + [dma((quads,)), dma((quads + 1,)), dma(()), dma(())] * 2,
+        + [dma(())] * 3
+        + [dma((2,))]
+        + [dma((quads,)), dma((2, quads + 1)), dma(()), dma(())] * 2,
         compiler_params=pltpu.CompilerParams(
             collective_id=0, has_side_effects=True, vmem_limit_bytes=32 * 1024 * 1024
         ),

time: 44.3 us -> 42.7 us (0.964)
  Pallas kernels: 43.5 us -> 41.9 us
    pallas_call x1, Pallas kernels: 42.4 us -> 40.8 us  [local(): pl.pallas_call(functools.partial(kernel, n_dp, n_seq), out_shape=held, in...]
where the time goes in v3:
time: 42.7 us; the launch traced here: 42.6 us
  Pallas kernels  41.9 us (98%)
  between operations  0.64 us (1%)
    pallas_call x1, Pallas kernels, local(): pl.pallas_call(functools.partial(kernel, n_dp, n_seq), out_shape=held, in...  40.8 us
    pallas_call x1, Pallas kernels, local(): pl.pallas_call(finish, out_shape=(wide, wide, wide, wide, jax.ShapeDtypeS...  1.07 us

profile of v3, /device:TPU:6, one launch (start us, length us, event | category | flops | bytes accessed | tf_op | source)
XLA Modules:
  0.0 42.6 jit_solution(9355001477570137103)
XLA Ops:
  0.6 40.8 %attention.1 = (bf16[1024,128]{1,0:T(8,128)(2,1)S(1)}, bf16[1024,128]{1,0:T(8,128)(2,1)S(1)}, f32[1024,128]{1,0:T(8,128)S(1)}, f32[1024,128]{1,0:T(8,128)S(1)}, ...) custom-call(bf16[1,1024,128]{2,1,0:T(8,128)(2,1)} %q_hbm.1, ...), custom_call_target="tpu_custom_call" | custom-call | tf_op jit(solution)/shard_map/attention/pallas_call | solution.py:391
  41.5 1.1 %finish.1 = (bf16[1,1024,128]{2,1,0:T(8,128)(2,1)}, bf16[1,1024,128]{2,1,0:T(8,128)(2,1)}, bf16[1,1024,128]{2,1,0:T(8,128)(2,1)}, bf16[1,1024,128]{2,1,0:T(8,128)(2,1)}, f32[32,384]{1,0:T(8,128)}) custom-call(bf16[1024,128]{1,0:T(8,128)(2,1)S(1)} %get-tuple-element.14.k, bf16[1024,128]{1,0:T(8,128)(2,1)S(1)} %get-tuple-element.15.v, ...), custom_call_target="tpu_custom_call" | custom-call | tf_op jit(solution)/shard_map/finish/pallas_call | solution.py:425

commit v4 on v3

--- a/solution.py
+++ b/solution.py
@@ -17,6 +17,7 @@
 LANES = 128
 X_PARTS = 2
 QUAD = 4
+SHIFT = 1
 PIECES = X_PARTS * QUAD
 
 
@@ -52,12 +53,13 @@
     me = lax.axis_index("seq")
     my_x = me // n_z
     my_z = me % n_z
-    my_quad = my_z // QUAD
-    my_piece = my_x * QUAD + my_z % QUAD
+    my_quad = lax.rem(my_z + SHIFT, n_z) // QUAD
+    my_piece = my_x * QUAD + lax.rem(my_z + SHIFT, QUAD)
     shard = gs.shape[1]
 
     def member(quad, piece):
-        return (piece // QUAD) * n_z + quad * QUAD + piece % QUAD
+        z = lax.rem(quad * QUAD + lax.rem(piece, QUAD) + n_z - SHIFT, n_z)
+        return (piece // QUAD) * n_z + z
 
     barrier = pltpu.get_barrier_semaphore()
 
@@ -144,24 +146,30 @@
 
     quads = n_z // QUAD
 
+    def before(source_quad, quad):
+        return (source_quad <= quad) | (quad == 0)
+
+    def after(source_quad, quad):
+        return (source_quad >= quad) | (source_quad == 0)
+
     def to_owners(source, target, send, recv, forward):
         free = my_x == (0 if forward else X_PARTS - 1)
         slot = jnp.where(free, 0, my_quad + 1)
 
         def one(x, z):
             device = (owner_dp, x * n_z + z)
-            quad = z // QUAD
+            quad = lax.rem(z + SHIFT, n_z) // QUAD
             if forward:
                 pltpu.make_async_remote_copy(
                     own_log, logs.at[side, me], log_send, log_recv.at[side],
                     device_id=device, device_id_type=MESH,
                 ).start()
-            needed = quad >= my_quad if forward else quad <= my_quad
+            needed = before(my_quad, quad) if forward else after(my_quad, quad)
 
             @pl.when(free | needed)
             def _():
                 pltpu.make_async_remote_copy(
-                    source.at[x * QUAD + lax.rem(z, QUAD)], target.at[side, me],
+                    source.at[x * QUAD + lax.rem(z + SHIFT, QUAD)], target.at[side, me],
                     send.at[quad], recv.at[side, slot],
                     device_id=device, device_id_type=MESH,
                 ).start()
@@ -183,7 +191,7 @@
     def owners_sent(target, send, forward):
         free = my_x == (0 if forward else X_PARTS - 1)
         for quad in range(quads):
-            needed = my_quad <= quad if forward else my_quad >= quad
+            needed = before(my_quad, quad) if forward else after(my_quad, quad)
             short = owning & (my_quad == quad)
 
             @pl.when((free | needed) & jnp.logical_not(short))
@@ -199,7 +207,7 @@
         wait_bytes(target.at[pl.ds(free * n_z, n_z)], recv.at[0])
         for quad in range(quads):
 
-            @pl.when(my_quad >= quad if forward else my_quad <= quad)
+            @pl.when(before(quad, my_quad) if forward else after(quad, my_quad))
             def _():
                 wait_bytes(
                     target.at[pl.ds((X_PARTS - 1 - free) * n_z + quad * QUAD, QUAD)],
@@ -322,8 +330,6 @@
         summed = summed + parts[device].astype(F32)
     gs[...] = summed
 
-    wait_bytes(outgoing, r2_recv)
-
     owners_sent(gathered, s1_send, True)
     owners_sent(gathered2, r1_send, False)
 
@@ -332,13 +338,17 @@
         wait_bytes(logs.at[0, pl.ds(0, n_seq - 1)], log_send)
         sent = pl.ds(0, 2 * PIECES - 1)
         wait_bytes(prefix.at[0, sent], s2_send)
-        wait_bytes(prefix2.at[0, sent], r2_send)
 
     @pl.when(jnp.logical_not(owning))
     def _():
         wait_bytes(logs.at[0], log_send)
 
     wait_bytes(parts.at[pl.ds(0, n_dp - 1)], part_send)
+    wait_bytes(outgoing, r2_recv)
+
+    @pl.when(owning)
+    def _():
+        wait_bytes(prefix2.at[0, pl.ds(0, 2 * PIECES - 1)], r2_send)
 
 
 def finish(

time: 42.7 us -> 42.4 us (level)
  Pallas kernels: 41.9 us -> 41.4 us
    pallas_call x1, Pallas kernels: 40.8 us -> 40.4 us  [local(): pl.pallas_call(functools.partial(kernel, n_dp, n_seq), out_shape=held, in...]
where the time goes in v4:
time: 42.4 us; the launch traced here: 42.1 us
  Pallas kernels  41.4 us (98%)
  between operations  0.64 us (2%)
    pallas_call x1, Pallas kernels, local(): pl.pallas_call(functools.partial(kernel, n_dp, n_seq), out_shape=held, in...  40.4 us
    pallas_call x1, Pallas kernels, local(): pl.pallas_call(finish, out_shape=(wide, wide, wide, wide, jax.ShapeDtypeS...  1.07 us

profile of v4, /device:TPU:6, one launch (start us, length us, event | category | flops | bytes accessed | tf_op | source)
XLA Modules:
  0.0 42.1 jit_solution(3480118552361285488)
XLA Ops:
  0.6 40.4 %attention.1 = (bf16[1024,128]{1,0:T(8,128)(2,1)S(1)}, bf16[1024,128]{1,0:T(8,128)(2,1)S(1)}, f32[1024,128]{1,0:T(8,128)S(1)}, f32[1024,128]{1,0:T(8,128)S(1)}, ...) custom-call(bf16[1,1024,128]{2,1,0:T(8,128)(2,1)} %q_hbm.1, ...), custom_call_target="tpu_custom_call" | custom-call | tf_op jit(solution)/shard_map/attention/pallas_call | solution.py:401
  41.0 1.1 %finish.1 = (bf16[1,1024,128]{2,1,0:T(8,128)(2,1)}, bf16[1,1024,128]{2,1,0:T(8,128)(2,1)}, bf16[1,1024,128]{2,1,0:T(8,128)(2,1)}, bf16[1,1024,128]{2,1,0:T(8,128)(2,1)}, f32[32,384]{1,0:T(8,128)}) custom-call(bf16[1024,128]{1,0:T(8,128)(2,1)S(1)} %get-tuple-element.14.k, bf16[1024,128]{1,0:T(8,128)(2,1)S(1)} %get-tuple-element.15.v, ...), custom_call_target="tpu_custom_call" | custom-call | tf_op jit(solution)/shard_map/finish/pallas_call | solution.py:435
